TPU v7x, 32 devices: a whole 2x2x4 slice. The times are simulated.
32 devices in a mesh: station: 4 (over z), group: 4 (over x, core), bias: 2 (over y).
Axes of the slice: x: 2, y: 2, z: 4, core: 2. Of those that a mesh axis runs over, the one named last changes fastest.
Arguments:
- normal_mat: float32 [128, 2304], P(('station', 'group')), may hold values from -16 to 18, as said below
- coupling: float32 [128, 2, 8, 48, 128], P(('station', 'group'), 'bias'), may hold values from -0.13258252 to 0.13258252
- lengths: int32 [128], P(('station', 'group')), may hold values from 12 to 48
- visible: int32 [128, 2, 8], P(('station', 'group'), 'bias'), may hold values from 0 to 16, as said below
- bias_prior: float32 [2, 16, 128], P('bias', 'station'), may hold values from 0.1 to 1
- unimod: int32 [128, 2304], P(('station', 'group')), may hold values from -1 to 2, as said below
Outputs:
- bias_cov: float32 [2, 16, 128, 128], P('bias', 'station')
- amb_cov: float32 [128, 2304], P(('station', 'group'))
Inputs may be any that keep to these rules, and one draw needn't show every extreme that they name: `normal_mat`: each station's matrix, read as 48 x 48 row by row, is symmetric with all eigenvalues 1 or more. Each list visible[s, h] holds distinct block numbers below 16 in its first slots and the value 16 in its unused slots; every list has at least one block; in every draw the stations of some devices use all 8 slots. `unimod`: each station's matrix, read as 48 x 48 row by row, is a unit lower triangular times a unit upper triangular integer matrix; each row of the lower factor and each column of the upper factor holds at most one entry off the diagonal, -1 or 1; so every leading square block has determinant 1.
All inputs are finite; a program needn't handle non-finite values.
Results may differ from a plain program's by a relative error of at most 0.0003.
Values sent between devices are 32-bit elements; how exact they have to be, the bound alone decides.
No kernel may reach another device: no remote copies, remote signals or barrier semaphores. Data moves between devices by JAX's collectives and lax.ppermute only.
A program may use at most 64 MiB of HBM per device.

v0:
```python
import jax
import jax.numpy as jnp
from jax import lax
from jax.sharding import PartitionSpec as P

NHALF = 16
precise = lax.Precision.HIGHEST


def spd_inverse(matrix):
    matrix_order = matrix.shape[-1]
    factor = jnp.linalg.cholesky(matrix)
    identity = jnp.broadcast_to(jnp.eye(matrix_order, dtype=matrix.dtype), matrix.shape)
    lower_inv = lax.linalg.triangular_solve(factor, identity, left_side=True, lower=True)
    return jnp.einsum("...ka,...kb->...ab", lower_inv, lower_inv, precision=precise)


def prepare(normal_mat, coupling, lengths):
    stations = coupling.shape[0]
    block_len = coupling.shape[3]
    positions = jnp.arange(block_len, dtype=jnp.int32)
    row_valid = (positions[None, :] < lengths[:, None]).astype(jnp.float32)
    keep_mask = row_valid[:, :, None] * row_valid[:, None, :]
    stacked = normal_mat.reshape(stations, block_len, block_len)
    effective = keep_mask * stacked + (1.0 - keep_mask) * jnp.eye(block_len, dtype=jnp.float32)
    inverse = spd_inverse(effective)
    weighted = coupling * row_valid[:, None, None, :, None]
    solved = jnp.einsum("sab,shjbc->shjac", inverse, weighted, precision=precise)
    return (keep_mask, inverse, weighted, solved)


def finish_cov(keep_mask, inverse, bias_part, unimod):
    stations = keep_mask.shape[0]
    block_len = keep_mask.shape[1]
    covariance = keep_mask * (inverse + bias_part)
    integer_map = unimod.reshape(stations, block_len, block_len).astype(jnp.float32)
    mapped = jnp.einsum("sab,sbc,sdc->sad", integer_map, covariance, integer_map, precision=precise)
    return (keep_mask * mapped).reshape(stations, block_len * block_len)


def local(normal_mat, coupling, lengths, visible, bias_prior, unimod):
    keep_mask, inverse, weighted, solved = prepare(normal_mat, coupling, lengths)
    reduced = jnp.einsum("shjac,shjad->shjcd", weighted, weighted - solved, precision=precise)
    block_width = coupling.shape[4]
    identity = jnp.eye(block_width, dtype=jnp.float32)
    columns = jnp.arange(NHALF, dtype=jnp.int32)
    selector = (visible[..., None] == columns).astype(jnp.float32)
    block_table = jnp.einsum("shjx,shjcd->hxcd", selector, reduced, precision=precise)
    local_sum = lax.psum_scatter(block_table, "station", scatter_dimension=1, tiled=True)
    block_sum = lax.psum(local_sum, "group")
    bias_cov = spd_inverse(block_sum + bias_prior[..., :, None] * identity)
    segment = lax.all_gather(bias_cov, "station", axis=1, tiled=True)
    piece_len = segment.shape[1]
    local_pick = (visible[..., None] == jnp.arange(piece_len, dtype=jnp.int32)).astype(jnp.float32)
    chosen = jnp.einsum("shjx,hxcd->shjcd", local_pick, segment, precision=precise)
    lifted = jnp.einsum("shjac,shjcd->shjad", solved, chosen, precision=precise)
    bias_part = jnp.einsum("shjad,shjbd->sab", lifted, solved, precision=precise)
    combined = lax.psum(bias_part.reshape(bias_part.shape[0], -1), "bias")
    amb_cov = finish_cov(keep_mask, inverse, combined.reshape(bias_part.shape), unimod)
    return (bias_cov, amb_cov)


def solution(mesh):
    return jax.shard_map(
        local,
        mesh=mesh,
        in_specs=(
            P(("station", "group"), None),
            P(("station", "group"), "bias", None, None, None),
            P(("station", "group")),
            P(("station", "group"), "bias", None),
            P("bias", "station", None),
            P(("station", "group"), None),
        ),
        out_specs=(P("bias", "station", None, None), P(("station", "group"), None)),
        check_vma=False,
    )
```

profile of v0, /device:TPU:0, one launch (start us, length us, event | category | flops | bytes accessed | tf_op | source)
XLA Modules:
  0.0 314.8 jit_solution(5613608994066356341)
XLA Ops:
  7.2 0.0 reduce-scatter.2.cloned.1.call-start
  7.3 0.7 fusion.43
  8.0 0.1 copy.56
  8.1 1.0 reshape.177
  9.1 0.1 copy.55
  9.2 0.0 copy-start
  9.2 0.1 fusion.24
  9.3 0.1 copy.57
  9.4 0.1 fusion.30
  9.6 35.2 %custom-call.14 = f32[8,48,48]{2,1,0:T(8,128)S(1)} custom-call(f32[8,48,48]{2,1,0:T(8,128)S(1)} %fusion.30), custom_call_target="Cholesky" | custom-call | tf_op jit(solution)/shard_map/jit(cholesky)/cholesky | solution.py:12
  44.8 0.1 compare_reduce_fusion
  44.9 0.1 select_bitcast_fusion.1
  45.0 29.5 %custom-call.15 = f32[8,1,48,48]{2,3,1,0:T(8,128)S(1)} custom-call(f32[8,1,48,48]{3,2,1,0:T(8,128)S(1)} %select_bitcast_fusion.1), custom_call_target="InvertDiagBlocksLowerTriangular" | custom-call | tf_op jit(solution)/shard_map/triangular_solve | solution.py:14
  74.6 0.5 fusion.28
  75.1 0.5 fusion.44
  75.6 0.0 copy-done
  75.6 1.7 fusion.10
  77.3 0.0 copy-start.2
  77.3 6.9 %fusion.7 = f32[8,8,128,128]{3,2,1,0:T(8,128)S(1)} fusion(f32[8,8,128,48]{2,3,1,0:T(8,128)S(1)} %fusion.10, f32[8,1,8,48,128]{4,3,2,1,0:T(8,128)S(1)} %copy-done, f32[8,48]{1,0:T(8,128)S(1)} %fusion.43), kind=kOutput, calls=%fused_computation.9 | convolution fusion | flops 605159424 | bytes 7341568 | tf_op jit(solution)/shard_map/shjac,shjad->shjcd/dot_general | solution.py:43
  84.2 0.0 copy-done.2
  84.2 4.1 %fusion.12 = f32[16,128,128]{2,0,1:T(8,128)S(1)} fusion(f32[8,8,128,128]{3,2,1,0:T(8,128)S(1)} %fusion.7, s32[8,8]{1,0:T(8,128)S(1)} %bitcast.86), kind=kOutput, calls=%fused_computation.14 | convolution fusion | flops 201327616 | bytes 5243136 | tf_op jit(solution)/shard_map/shjx,shjcd->hxcd/dot_general | solution.py:48
  88.3 0.0 copy-start.3
  88.3 1.4 copy.62
  89.8 0.0 reduce-scatter.2.cloned.1.call-update
  89.8 0.0 all-reduce.3.cloned.1.call-start
  89.9 30.1 %reduce-scatter.2.cloned.1.call-done = f32[1,4,128,128]{2,3,1,0:T(8,128)} async-done(((f32[1,16,128,128]{2,3,1,0:T(8,128)}), f32[1,4,128,128]{2,3,1,0:T(8,128)}) %reduce-scatter.2.cloned.1.call-update) | async-done | bytes 262160 | tf_op jit(solution)/shard_map/reduce_scatter | solution.py:49
  120.0 0.0 all-reduce.3.cloned.1.call-update
  120.0 0.0 all-gather.3.cloned.1.call-start
  120.1 0.1 copy.63
  120.2 32.9 %all-reduce.3.cloned.1.call-done = f32[1,4,128,128]{2,3,1,0:T(8,128)} async-done(((f32[1,4,128,128]{2,3,1,0:T(8,128)}), f32[1,4,128,128]{2,3,1,0:T(8,128)}) %all-reduce.3.cloned.1.call-update) | async-done | bytes 262160 | tf_op jit(solution)/shard_map/psum | solution.py:50
  153.1 0.0 copy-done.3
  153.1 1.0 multiply_add_fusion
  154.1 0.1 copy.64
  154.2 1.0 fusion.23
  155.3 46.9 %custom-call.16 = f32[1,4,128,128]{3,2,1,0:T(8,128)S(1)} custom-call(f32[1,4,128,128]{3,2,1,0:T(8,128)S(1)} %fusion.23), custom_call_target="Cholesky" | custom-call | tf_op jit(solution)/shard_map/jit(cholesky)/cholesky | solution.py:12
  202.2 0.1 compare_reduce_fusion.1
  202.3 0.1 select_bitcast_fusion
  202.4 39.3 %custom-call.17 = f32[1,4,1,128,128]{3,4,2,1,0:T(8,128)S(1)} custom-call(f32[1,4,1,128,128]{4,3,2,1,0:T(8,128)S(1)} %select_bitcast_fusion), custom_call_target="InvertDiagBlocksLowerTriangular" | custom-call | tf_op jit(solution)/shard_map/triangular_solve | solution.py:14
  241.8 0.6 fusion.21
  242.3 1.3 fusion.45
  243.7 0.0 all-gather.3.cloned.1.call-update
  243.7 0.3 all-reduce.5.cloned.1.call-start
  243.9 27.9 %all-gather.3.cloned.1.call-done = f32[16,128,128]{2,1,0:T(8,128)} async-done(((f32[4,128,128]{2,1,0:T(8,128)}), f32[16,128,128]{2,1,0:T(8,128)}) %all-gather.3.cloned.1.call-update) | async-done | bytes 1048592 | tf_op jit(solution)/shard_map/all_gather | solution.py:52
  271.8 3.3 %convolution_bitcast_fusion = f32[8,8,128,128]{3,1,0,2:T(8,128)S(1)} fusion(f32[16,128,128,1]{2,1,0,3:T(8,128)} %bitcast.85, s32[8,8]{1,0:T(8,128)S(1)} %bitcast.87), kind=kOutput, calls=%fused_computation.4 | convolution fusion | flops 201327616 | bytes 5243136 | tf_op jit(solution)/shard_map/shjx,hxcd->shjcd/dot_general | solution.py:55
  275.1 6.0 %fusion = f32[8,8,48,128]{3,2,1,0:T(8,128)S(1)} fusion(f32[8,8,128,48]{2,3,1,0:T(8,128)S(1)} %fusion.10, f32[8,8,128,128]{3,1,0,2:T(8,128)S(1)} %convolution_bitcast_fusion), kind=kOutput, calls=%fused_computation | convolution fusion | flops 603979776 | bytes 7340032 | tf_op jit(solution)/shard_map/shjac,shjcd->shjad/dot_general | solution.py:56
  281.1 0.0 copy-start.1
  281.1 2.4 fusion.15
  283.5 0.0 all-reduce.5.cloned.1.call-update
  283.5 0.1 copy.70
  283.6 0.0 copy-done.1
  283.7 0.1 convert_element_type.47
  283.8 21.7 %all-reduce.5.cloned.1.call-done = f32[8,48,48]{1,2,0:T(8,128)} async-done(((f32[8,48,48]{1,2,0:T(8,128)}), f32[8,48,48]{1,2,0:T(8,128)}) %all-reduce.5.cloned.1.call-update) | async-done | bytes 73744 | tf_op jit(solution)/shard_map/psum | solution.py:58
  305.5 1.4 fusion.26
  306.9 0.4 convolution_multiply_fusion
  307.4 0.1 copy.73
  307.5 0.8 reshape.185
  (9 shorter events, 0.2 us)
Async XLA Ops:
  7.2 112.8 %reduce-scatter.2.cloned.1.call-start = ((), (), s32[]{:S(2)}) async-start(), calls=%async_computation.1 | async-start | bytes 1310720 | tf_op jit(solution)/shard_map/reduce_scatter | solution.py:49
  9.2 66.4 %copy-start = (f32[8,1,8,48,128]{4,3,2,1,0:T(8,128)S(1)}, f32[8,1,8,48,128]{4,3,2,1,0:T(8,128)}, u32[]{:S(2)}) copy-start(f32[8,1,8,48,128]{4,3,2,1,0:T(8,128)} %param.7) | copy-start | bytes 4718596
  77.3 6.9 %copy-start.2 = (s32[8,1,8]{2,1,0:T(1,128)S(1)}, s32[8,1,8]{2,1,0:T(1,128)}, u32[]{:S(2)}) copy-start(s32[8,1,8]{2,1,0:T(1,128)} %param.9) | copy-start | bytes 772
  88.3 64.8 %copy-start.3 = (f32[1,4,128]{2,1,0:T(4,128)S(1)}, f32[1,4,128]{2,1,0:T(4,128)}, u32[]{:S(2)}) copy-start(f32[1,4,128]{2,1,0:T(4,128)} %param.10) | copy-start | bytes 6148
  89.8 63.3 %all-reduce.3.cloned.1.call-start = ((), (), s32[]{:S(2)}) async-start(), calls=%async_computation.2 | async-start | bytes 524288 | tf_op jit(solution)/shard_map/psum | solution.py:50
  120.0 151.8 %all-gather.3.cloned.1.call-start = ((), (), s32[]{:S(2)}) async-start(), calls=%async_computation.4 | async-start | bytes 1310720 | tf_op jit(solution)/shard_map/all_gather | solution.py:52
  243.7 61.8 %all-reduce.5.cloned.1.call-start = ((), (), s32[]{:S(2)}) async-start(), calls=%async_computation.3 | async-start | bytes 393216 | tf_op jit(solution)/shard_map/psum | solution.py:58
  281.1 2.5 copy-start.1
Sparse Core Ops, SparseCore 0:
  89.9 29.9 reduce-scatter.1
  122.3 30.7 all-reduce.2
  243.8 27.9 all-gather.2
  283.6 21.7 all-reduce.4
where the time goes:
time: 315 us
  other arithmetic  154 us (49%)
  waiting for transfers between devices  113 us (36%)
  matrix products  29.1 us (9%)
  between operations  14.1 us (4%)
  local copies, waits for them, and re-layouts  4.08 us (1%)
    another operation x8, other arithmetic, spd_inverse(): factor = jnp.linalg.cholesky(matrix)  82.4 us
    another operation x6, other arithmetic, spd_inverse(): lax.linalg.triangular_solve(factor, identity, left_side=True, lower=True)  69.1 us
    psum x1, waiting for transfers between devices, local(): block_sum = lax.psum(local_sum, 'group')  32.9 us
    reduce_scatter x1, waiting for transfers between devices, local(): lax.psum_scatter(block_table, 'station', scatter_dimension=1, tiled=True)  30.1 us
    all_gather x1, waiting for transfers between devices, local(): segment = lax.all_gather(bias_cov, 'station', axis=1, tiled=True)  27.9 us
    psum x1, waiting for transfers between devices, local(): combined = lax.psum(bias_part.reshape(bias_part.shape[0], -1), 'bias')  21.7 us
    dot_general x1, matrix products, local(): jnp.einsum('shjac,shjad->shjcd', weighted, weighted - solved, precision=p...  6.89 us
  transfers between devices with their start and end apart: 4, of which 4 were waited for; matrix products, arithmetic and copies ran while one was open for 0% of the time, Pallas kernels for 0%

commit v1 on v0

--- a/solution.py
+++ b/solution.py
@@ -47,7 +47,14 @@
     selector = (visible[..., None] == columns).astype(jnp.float32)
     block_table = jnp.einsum("shjx,shjcd->hxcd", selector, reduced, precision=precise)
     local_sum = lax.psum_scatter(block_table, "station", scatter_dimension=1, tiled=True)
-    block_sum = lax.psum(local_sum, "group")
+    n_peers_all = jax.lax.axis_size("group")
+    block_sum, near = (local_sum, 0)
+    while 1 << near < n_peers_all:
+        fresh = jax.lax.ppermute(
+            block_sum, "group", [(i0, i0 ^ 1 << near) for i0 in range(n_peers_all)]
+        )
+        block_sum = block_sum + fresh
+        near = near + 1
     bias_cov = spd_inverse(block_sum + bias_prior[..., :, None] * identity)
     segment = lax.all_gather(bias_cov, "station", axis=1, tiled=True)
     piece_len = segment.shape[1]

time: 315 us -> 290 us (0.921)
  waiting for transfers between devices: 113 us -> 86.7 us
    psum x1 -> x0, waiting for transfers between devices: 32.9 us -> none  [local(): block_sum = lax.psum(local_sum, 'group')]
    ppermute x0 -> x2, waiting for transfers between devices: none -> 8.46 us  [local(): jax.lax.ppermute(block_sum, 'group', [(i0, i0 ^ 1 << near) for i0 in rang...]
  transfers between devices with their start and end apart: 4 -> 5, of which waited for: 4 -> 5; matrix products, arithmetic and copies ran while one was open for 0% -> 0% of each run, Pallas kernels for 0% -> 0%
where the time goes in v1:
time: 290 us; the launch traced here: 289 us
  other arithmetic  154 us (53%)
  waiting for transfers between devices  86.7 us (30%)
  matrix products  29.1 us (10%)
  between operations  14 us (5%)
  local copies, waits for them, and re-layouts  4.08 us (1%)
    another operation x8, other arithmetic, spd_inverse(): factor = jnp.linalg.cholesky(matrix)  82.4 us
    another operation x6, other arithmetic, spd_inverse(): lax.linalg.triangular_solve(factor, identity, left_side=True, lower=True)  69.1 us
    reduce_scatter x1, waiting for transfers between devices, local(): lax.psum_scatter(block_table, 'station', scatter_dimension=1, tiled=True)  30.1 us
    all_gather x1, waiting for transfers between devices, local(): segment = lax.all_gather(bias_cov, 'station', axis=1, tiled=True)  26.4 us
    psum x1, waiting for transfers between devices, local(): combined = lax.psum(bias_part.reshape(bias_part.shape[0], -1), 'bias')  21.7 us
    ppermute x2, waiting for transfers between devices, local(): jax.lax.ppermute(block_sum, 'group', [(i0, i0 ^ 1 << near) for i0 in rang...  8.46 us
    dot_general x1, matrix products, local(): jnp.einsum('shjac,shjad->shjcd', weighted, weighted - solved, precision=p...  6.89 us
    dot_general x1, matrix products, local(): lifted = jnp.einsum('shjac,shjcd->shjad', solved, chosen, precision=precise)  5.97 us
  transfers between devices with their start and end apart: 5, of which 5 were waited for; matrix products, arithmetic and copies ran while one was open for 0% of the time, Pallas kernels for 0%

profile of v1, /device:TPU:0, one launch (start us, length us, event | category | flops | bytes accessed | tf_op | source)
XLA Modules:
  0.0 289.4 jit_solution(2880634829708052729)
XLA Ops:
  7.2 0.0 reduce-scatter.2.cloned.1.call-start
  7.3 0.7 fusion.43
  8.0 0.1 copy.56
  8.1 1.0 reshape.177
  9.1 0.1 copy.55
  9.2 0.0 copy-start
  9.2 0.1 fusion.24
  9.3 0.1 copy.57
  9.4 0.1 fusion.30
  9.6 35.2 %custom-call.14 = f32[8,48,48]{2,1,0:T(8,128)S(1)} custom-call(f32[8,48,48]{2,1,0:T(8,128)S(1)} %fusion.30), custom_call_target="Cholesky" | custom-call | tf_op jit(solution)/shard_map/jit(cholesky)/cholesky | solution.py:12
  44.8 0.1 compare_reduce_fusion
  44.9 0.1 select_bitcast_fusion.1
  45.0 29.5 %custom-call.15 = f32[8,1,48,48]{2,3,1,0:T(8,128)S(1)} custom-call(f32[8,1,48,48]{3,2,1,0:T(8,128)S(1)} %select_bitcast_fusion.1), custom_call_target="InvertDiagBlocksLowerTriangular" | custom-call | tf_op jit(solution)/shard_map/triangular_solve | solution.py:14
  74.6 0.5 fusion.28
  75.1 0.5 fusion.44
  75.6 0.0 copy-done
  75.6 1.7 fusion.10
  77.3 0.0 copy-start.2
  77.3 6.9 %fusion.7 = f32[8,8,128,128]{3,2,1,0:T(8,128)S(1)} fusion(f32[8,8,128,48]{2,3,1,0:T(8,128)S(1)} %fusion.10, f32[8,1,8,48,128]{4,3,2,1,0:T(8,128)S(1)} %copy-done, f32[8,48]{1,0:T(8,128)S(1)} %fusion.43), kind=kOutput, calls=%fused_computation.9 | convolution fusion | flops 605159424 | bytes 7341568 | tf_op jit(solution)/shard_map/shjac,shjad->shjcd/dot_general | solution.py:43
  84.2 0.0 copy-done.2
  84.2 4.1 %fusion.12 = f32[16,128,128]{2,0,1:T(8,128)S(1)} fusion(f32[8,8,128,128]{3,2,1,0:T(8,128)S(1)} %fusion.7, s32[8,8]{1,0:T(8,128)S(1)} %bitcast.86), kind=kOutput, calls=%fused_computation.14 | convolution fusion | flops 201327616 | bytes 5243136 | tf_op jit(solution)/shard_map/shjx,shjcd->hxcd/dot_general | solution.py:48
  88.3 0.0 copy-start.3
  88.3 1.4 copy.62
  89.8 0.0 reduce-scatter.2.cloned.1.call-update
  89.8 0.0 all-gather.3.cloned.1.call-start
  89.9 30.1 %reduce-scatter.2.cloned.1.call-done = f32[1,4,128,128]{2,3,1,0:T(8,128)} async-done(((f32[1,16,128,128]{2,3,1,0:T(8,128)}), f32[1,4,128,128]{2,3,1,0:T(8,128)}) %reduce-scatter.2.cloned.1.call-update) | async-done | bytes 262160 | tf_op jit(solution)/shard_map/reduce_scatter | solution.py:49
  120.0 0.0 collective-permute-start
  120.0 1.7 collective-permute-done
  121.7 1.0 add.43
  122.7 1.5 collective-permute-start.1
  124.3 0.1 copy.63
  124.4 6.7 %collective-permute-done.1 = f32[1,4,128,128]{2,3,1,0:T(8,128)S(1)} collective-permute-done((f32[1,4,128,128]{2,3,1,0:T(8,128)S(1)}, f32[1,4,128,128]{2,3,1,0:T(8,128)S(1)}, u32[]{:S(2)}, u32[]{:S(2)}) %collective-permute-start.1) | collective-permute-done | bytes 262176 | tf_op jit(solution)/shard_map/ppermute | solution.py:53
  131.1 0.0 copy-done.3
  131.2 0.1 copy.64
  131.3 46.9 %custom-call.16 = f32[1,4,128,128]{3,2,1,0:T(8,128)S(1)} custom-call(f32[1,4,128,128]{3,2,1,0:T(8,128)S(1)} %fusion.23), custom_call_target="Cholesky" | custom-call | tf_op jit(solution)/shard_map/jit(cholesky)/cholesky | solution.py:12
  178.3 0.1 compare_reduce_fusion.1
  178.4 0.1 select_bitcast_fusion
  178.5 39.3 %custom-call.17 = f32[1,4,1,128,128]{3,4,2,1,0:T(8,128)S(1)} custom-call(f32[1,4,1,128,128]{4,3,2,1,0:T(8,128)S(1)} %select_bitcast_fusion), custom_call_target="InvertDiagBlocksLowerTriangular" | custom-call | tf_op jit(solution)/shard_map/triangular_solve | solution.py:14
  217.8 0.6 fusion.21
  218.4 1.3 fusion.45
  219.7 0.0 all-gather.3.cloned.1.call-update
  219.7 0.3 all-reduce.2.cloned.1.call-start
  220.0 26.4 %all-gather.3.cloned.1.call-done = f32[16,128,128]{2,1,0:T(8,128)} async-done(((f32[4,128,128]{2,1,0:T(8,128)}), f32[16,128,128]{2,1,0:T(8,128)}) %all-gather.3.cloned.1.call-update) | async-done | bytes 1048592 | tf_op jit(solution)/shard_map/all_gather | solution.py:59
  246.4 3.3 %convolution_bitcast_fusion = f32[8,8,128,128]{3,1,0,2:T(8,128)S(1)} fusion(f32[16,128,128,1]{2,1,0,3:T(8,128)} %bitcast.85, s32[8,8]{1,0:T(8,128)S(1)} %bitcast.87), kind=kOutput, calls=%fused_computation.4 | convolution fusion | flops 201327616 | bytes 5243136 | tf_op jit(solution)/shard_map/shjx,hxcd->shjcd/dot_general | solution.py:62
  249.7 6.0 %fusion = f32[8,8,48,128]{3,2,1,0:T(8,128)S(1)} fusion(f32[8,8,128,48]{2,3,1,0:T(8,128)S(1)} %fusion.10, f32[8,8,128,128]{3,1,0,2:T(8,128)S(1)} %convolution_bitcast_fusion), kind=kOutput, calls=%fused_computation | convolution fusion | flops 603979776 | bytes 7340032 | tf_op jit(solution)/shard_map/shjac,shjcd->shjad/dot_general | solution.py:63
  255.7 0.0 copy-start.1
  255.7 2.4 fusion.15
  258.1 0.0 all-reduce.2.cloned.1.call-update
  258.1 0.1 copy.70
  258.2 0.0 copy-done.1
  258.3 0.1 convert_element_type.47
  258.4 21.7 %all-reduce.2.cloned.1.call-done = f32[8,48,48]{1,2,0:T(8,128)} async-done(((f32[8,48,48]{1,2,0:T(8,128)}), f32[8,48,48]{1,2,0:T(8,128)}) %all-reduce.2.cloned.1.call-update) | async-done | bytes 73744 | tf_op jit(solution)/shard_map/psum | solution.py:65
  280.1 1.4 fusion.26
  281.5 0.4 convolution_multiply_fusion
  281.9 0.1 copy.73
  282.1 0.8 reshape.185
  (11 shorter events, 0.2 us)
Async XLA Ops:
  7.2 112.8 %reduce-scatter.2.cloned.1.call-start = ((), (), s32[]{:S(2)}) async-start(), calls=%async_computation.1 | async-start | bytes 1310720 | tf_op jit(solution)/shard_map/reduce_scatter | solution.py:49
  9.2 66.4 %copy-start = (f32[8,1,8,48,128]{4,3,2,1,0:T(8,128)S(1)}, f32[8,1,8,48,128]{4,3,2,1,0:T(8,128)}, u32[]{:S(2)}) copy-start(f32[8,1,8,48,128]{4,3,2,1,0:T(8,128)} %param.7) | copy-start | bytes 4718596
  77.3 6.9 %copy-start.2 = (s32[8,1,8]{2,1,0:T(1,128)S(1)}, s32[8,1,8]{2,1,0:T(1,128)}, u32[]{:S(2)}) copy-start(s32[8,1,8]{2,1,0:T(1,128)} %param.9) | copy-start | bytes 772
  88.3 42.8 %copy-start.3 = (f32[1,4,128]{2,1,0:T(4,128)S(1)}, f32[1,4,128]{2,1,0:T(4,128)}, u32[]{:S(2)}) copy-start(f32[1,4,128]{2,1,0:T(4,128)} %param.10) | copy-start | bytes 6148
  89.8 156.6 %all-gather.3.cloned.1.call-start = ((), (), s32[]{:S(2)}) async-start(), calls=%async_computation.3 | async-start | bytes 1310720 | tf_op jit(solution)/shard_map/all_gather | solution.py:59
  120.0 1.7 collective-permute-start
  122.7 8.4 %collective-permute-start.1 = (f32[1,4,128,128]{2,3,1,0:T(8,128)S(1)}, f32[1,4,128,128]{2,3,1,0:T(8,128)S(1)}, u32[]{:S(2)}, u32[]{:S(2)}) collective-permute-start(f32[1,4,128,128]{2,3,1,0:T(8,128)S(1)} %add.43), channel_id=1, source_target_pairs={{0,4},{2,6},{4,0},{6,2},{1,5},{3,7},{5,1},{7,3},{8,12},{10,14},{12... | collective-permute-start | bytes 786440 | tf_op jit(solution)/shard_map/ppermute | solution.py:53
  219.7 60.3 %all-reduce.2.cloned.1.call-start = ((), (), s32[]{:S(2)}) async-start(), calls=%async_computation.2 | async-start | bytes 393216 | tf_op jit(solution)/shard_map/psum | solution.py:65
  255.7 2.5 copy-start.1
Sparse Core Ops, SparseCore 0:
  89.9 29.9 reduce-scatter.1
  219.9 26.4 all-gather.2
  258.2 21.7 all-reduce.1
